TPU v7x, 32 devices: a whole 2x2x4 slice. The times are simulated.
32 devices in a mesh: group: 4 (over y, x), shard: 8 (over z, core).
Axes of the slice: x: 2, y: 2, z: 4, core: 2. Of those that a mesh axis runs over, the one named last changes fastest.
Arguments:
- entity: float32 [16384, 400], P(('group', 'shard')), may hold values from -6 to 6
- entity_state: float32 [16384], P(('group', 'shard')), may hold values from 0.1 to 10
- relation: float32 [1345, 400], replicated, may hold values from -6 to 6
- relation_state: float32 [1345], replicated, may hold values from 10 to 1000
- src_send: int32 [32, 8, 128], P(('group', 'shard')), may hold values from 0 to 511
- dst_send: int32 [32, 8, 128], P(('group', 'shard')), may hold values from 0 to 511
- edge_source: int32 [32768], P(('group', 'shard')), may hold values from 0 to 1023
- edge_relation: int32 [32768], P(('group', 'shard')), may hold values from 0 to 1344
- edge_target: int32 [32768], P(('group', 'shard')), may hold values from 0 to 1023
- neg_slots: int32 [64, 1000], P(('group', 'shard')), may hold values from 0 to 1023
- edge_count: int32 [32], P(('group', 'shard')), may hold values from 1 to 1024, 10922 in all
Outputs:
- entity_new: float32 [16384, 400], P(('group', 'shard'))
- relation_new: float32 [1345, 400], replicated
- edge_loss: float32 [32768], P(('group', 'shard'))
Inputs may be any that keep to these rules, and one draw needn't show every extreme that they name: The live edges of a device are its first edge_count slots; some device has all 1024 live.
All inputs are finite; a program needn't handle non-finite values.
Results may differ from a plain program's by a relative error of at most 0.0003.
Values sent between devices are 32-bit elements; how exact they have to be, the bound alone decides.
No kernel may reach another device: no remote copies, remote signals or barrier semaphores. Data moves between devices by JAX's collectives and lax.ppermute only.
A program may use at most 128 MiB of HBM per device.

v0:
```python
import jax
import jax.numpy as jnp
from jax import lax
from jax.sharding import PartitionSpec as P

SPAN = 512
learn_rate = 0.5


def passed_along(value, axis, by):
    count = lax.axis_size(axis)
    return lax.ppermute(value, axis, [(i, (i + by) % count) for i in range(count)])


def complex_product(multiplier, multiplicand):
    half_width = multiplier.shape[1] // 2
    first_real, first_imag = (multiplier[:, :half_width], multiplier[:, half_width:])
    second_real, second_imag = (multiplicand[:, :half_width], multiplicand[:, half_width:])
    return jnp.concatenate(
        [
            first_real * second_real - first_imag * second_imag,
            first_real * second_imag + first_imag * second_real,
        ],
        axis=1,
    )


def conj_product(multiplier, multiplicand):
    half_width = multiplier.shape[1] // 2
    first_real, first_imag = (multiplier[:, :half_width], multiplier[:, half_width:])
    second_real, second_imag = (multiplicand[:, :half_width], multiplicand[:, half_width:])
    return jnp.concatenate(
        [
            first_real * second_real + first_imag * second_imag,
            first_imag * second_real - first_real * second_imag,
        ],
        axis=1,
    )


def span_terms(queries, tail_rows, negatives, live_mask):
    pos_score = jnp.sum(queries * tail_rows, axis=1)
    neg_score = jnp.dot(queries, negatives.T, precision=lax.Precision.HIGHEST)
    score_peak = jnp.maximum(pos_score, jnp.max(neg_score, axis=1))
    exp_total = jnp.exp(pos_score - score_peak) + jnp.sum(
        jnp.exp(neg_score - score_peak[:, None]), axis=1
    )
    log_total = score_peak + jnp.log(exp_total)
    edge_loss = (log_total - pos_score) * live_mask
    pos_grad = (jnp.exp(pos_score - log_total) - 1.0) * live_mask
    neg_grad = jnp.exp(neg_score - log_total[:, None]) * live_mask[:, None]
    neg_query = jnp.dot(neg_grad, negatives, precision=lax.Precision.HIGHEST)
    negative_grad = lax.dot_general(
        neg_grad, queries, (((0,), (0,)), ((), ())), precision=lax.Precision.HIGHEST
    )
    return (edge_loss, pos_grad, neg_query, negative_grad)


def adagrad(params, accumulator, gradient):
    new_state = accumulator + jnp.mean(gradient * gradient, axis=1)
    return params - learn_rate * gradient / jnp.sqrt(new_state)[:, None]


def on_device(
    entity,
    entity_state,
    relation,
    relation_state,
    src_send,
    dst_send,
    edge_source,
    edge_relation,
    edge_target,
    neg_slots,
    edge_count,
):
    feature_count = entity.shape[1]
    peer_count, block_size = (src_send.shape[1], src_send.shape[2])
    table_rows = peer_count * block_size
    edge_rows = edge_source.shape[0]
    spans = edge_rows // SPAN
    sent_source = lax.all_to_all(
        entity[src_send[0]], "shard", split_axis=0, concat_axis=0, tiled=True
    )
    source_table = sent_source.reshape(table_rows, feature_count)
    shifted = passed_along(entity[dst_send[0]], "group", -1)
    target_blocks = lax.all_to_all(shifted, "shard", split_axis=0, concat_axis=0, tiled=True)
    target_table = target_blocks.reshape(table_rows, feature_count)
    live_count = edge_count[0]
    live_mask = (jnp.arange(edge_rows, dtype=jnp.int32) < live_count).astype(jnp.float32)
    head_rows = source_table[edge_source]
    tail_rows = target_table[edge_target]
    rel_rows = relation[edge_relation]
    queries = complex_product(head_rows, rel_rows)

    def span_turn(position, carried):
        loss_all, pos_all, query_all, target_grad = carried
        first_row = position * SPAN
        slots = neg_slots[position]
        edge_loss, pos_grad, neg_query, negative_grad = span_terms(
            lax.dynamic_slice_in_dim(queries, first_row, SPAN),
            lax.dynamic_slice_in_dim(tail_rows, first_row, SPAN),
            target_table[slots],
            lax.dynamic_slice_in_dim(live_mask, first_row, SPAN),
        )
        loss_all = lax.dynamic_update_slice_in_dim(loss_all, edge_loss, first_row, 0)
        pos_all = lax.dynamic_update_slice_in_dim(pos_all, pos_grad, first_row, 0)
        query_all = lax.dynamic_update_slice_in_dim(query_all, neg_query, first_row, 0)
        target_grad = target_grad.at[slots].add(negative_grad)
        return (loss_all, pos_all, query_all, target_grad)

    initial = (
        jnp.zeros((edge_rows,), jnp.float32),
        jnp.zeros((edge_rows,), jnp.float32),
        jnp.zeros((edge_rows, feature_count), jnp.float32),
        jnp.zeros((table_rows, feature_count), jnp.float32),
    )
    edge_loss, pos_grad, neg_query, target_grad = lax.fori_loop(0, spans, span_turn, initial)
    query_grad = pos_grad[:, None] * tail_rows + neg_query
    target_grad = target_grad.at[edge_target].add(pos_grad[:, None] * queries)
    source_grad = (
        jnp.zeros((table_rows, feature_count), jnp.float32)
        .at[edge_source]
        .add(conj_product(query_grad, rel_rows))
    )
    relation_part = (
        jnp.zeros(relation.shape, jnp.float32)
        .at[edge_relation]
        .add(conj_product(query_grad, head_rows))
    )
    relation_total = lax.psum(relation_part, ("group", "shard"))
    returned_source = lax.all_to_all(
        source_grad.reshape(peer_count, block_size, feature_count),
        "shard",
        split_axis=0,
        concat_axis=0,
        tiled=True,
    )
    entity_grad = (
        jnp.zeros(entity.shape, jnp.float32)
        .at[src_send[0].reshape(-1)]
        .add(returned_source.reshape(-1, feature_count))
    )
    target_blocks_grad = target_grad.reshape(peer_count, block_size, feature_count)
    returned_blocks = lax.all_to_all(
        target_blocks_grad, "shard", split_axis=0, concat_axis=0, tiled=True
    )
    home_blocks = passed_along(returned_blocks, "group", 1)
    entity_grad = entity_grad.at[dst_send[0].reshape(-1)].add(
        home_blocks.reshape(-1, feature_count)
    )
    return (
        adagrad(entity, entity_state, entity_grad),
        adagrad(relation, relation_state, relation_total),
        edge_loss,
    )


def solution(mesh):
    return jax.shard_map(
        on_device,
        mesh=mesh,
        in_specs=(
            P(("group", "shard"), None),
            P(("group", "shard")),
            P(),
            P(),
            P(("group", "shard"), None, None),
            P(("group", "shard"), None, None),
            P(("group", "shard")),
            P(("group", "shard")),
            P(("group", "shard")),
            P(("group", "shard"), None),
            P(("group", "shard")),
        ),
        out_specs=(P(("group", "shard"), None), P(), P(("group", "shard"))),
        check_vma=False,
    )
```

profile of v0, /device:TPU:0, one launch (start us, length us, event | category | flops | bytes accessed | tf_op | source)
XLA Modules:
  0.0 453.2 jit_solution(17644259954135910867)
XLA Ops:
  14.6 6.5 %all-to-all-start = ((f32[8,128,400]{1,2,0:T(8,128)}), f32[8,128,400]{1,2,0:T(8,128)}, u32[]{:S(2)}, u32[]{:S(2)}) async-start(f32[8,128,400]{1,2,0:T(8,128)} %copy.47), calls=%async_computation | async-start | bytes 3276800 | tf_op jit(solution)/shard_map/all_to_all | solution.py:82
  28.8 36.1 %collective-permute-done = f32[8,128,400]{1,2,0:T(8,128)} collective-permute-done((f32[8,128,400]{1,2,0:T(8,128)}, f32[8,128,400]{1,2,0:T(8,128)}, u32[]{:S(2)}, u32[]{:S(2)}) %collective-permute-start) | collective-permute-done | bytes 1638432 | tf_op jit(solution)/shard_map/ppermute | solution.py:12
  64.9 4.7 %all-to-all-start.1 = ((f32[8,128,400]{1,2,0:T(8,128)}), f32[8,128,400]{1,2,0:T(8,128)}, u32[]{:S(2)}, u32[]{:S(2)}) async-start(f32[8,128,400]{1,2,0:T(8,128)} %collective-permute-done), calls=%async_computation.1 | async-start | bytes 3276800 | tf_op jit(solution)/shard_map/all_to_all | solution.py:87
  72.9 4.9 %gather_fusion.3 = f32[1024,400]{1,0:T(8,128)} fusion(f32[1345,400]{1,0:T(8,128)S(1)} %copy.49, s32[1024]{0:T(1024)S(1)} %get-tuple-element.335), kind=kCustom, calls=%fused_computation.3 | custom fusion | bytes 3280896 | tf_op jit(solution)/shard_map/gather | solution.py:93
  79.6 4.9 %gather_fusion.2 = f32[1024,400]{1,0:T(8,128)} fusion(f32[1024,400]{1,0:T(8,128)S(1)} %bitcast.42, s32[1024]{0:T(1024)S(1)} %get-tuple-element.338), kind=kCustom, calls=%fused_computation.2 | custom fusion | bytes 3280896 | tf_op jit(solution)/shard_map/gather | solution.py:91
  90.5 18.4 %all-to-all-done.1 = f32[8,128,400]{1,2,0:T(8,128)} async-done(((f32[8,128,400]{1,2,0:T(8,128)}), f32[8,128,400]{1,2,0:T(8,128)}, u32[]{:S(2)}, u32[]{:S(2)}) %all-to-all-start.1) | async-done | bytes 1638432 | tf_op jit(solution)/shard_map/all_to_all | solution.py:87
  110.8 4.9 %gather_fusion.5 = f32[1024,400]{1,0:T(8,128)} fusion(f32[1024,400]{1,0:T(8,128)S(1)} %bitcast.39, s32[1024]{0:T(1024)S(1)} %get-tuple-element.337), kind=kCustom, calls=%fused_computation.5 | custom fusion | bytes 3280896 | tf_op jit(solution)/shard_map/gather | solution.py:92
  118.7 68.8 %while.21 = (s32[]{:T(128)}, f32[1024]{0:T(1024)S(1)}, f32[1024]{0:T(1024)S(1)}, f32[1024,400]{0,1:T(8,128)}, f32[1024,400]{1,0:T(8,128)}, /*index=5*/f32[1024,4...) while((s32[]{:T(128)}, f32[1024]{0:T(1024)S(1)}, ...), condition=%wide.region_5.0_spmd, body=%wide.region_0.0_spmd.sunk | while | flops 7377200640 | bytes 52573032 | solution.py:118
  120.9 4.9 %gather_fusion = f32[1000,400]{1,0:T(8,128)} fusion(f32[1024,400]{1,0:T(8,128)S(1)} %get-tuple-element.447, s32[1024]{0:T(1024)S(1)} %pad_clamp_fusion.2), kind=kCustom, calls=%fused_computation.clone.1 | custom fusion | bytes 3204000 | tf_op jit(solution)/shard_map/while/body/eval_jaxpr/gather | solution.py:103
  125.8 5.4 %fusion.44 = (f32[512]{0:T(512)S(1)}, f32[512,1000]{0,1:T(8,128)S(1)}) fusion(f32[1000,400]{1,0:T(8,128)} %gather_fusion, f32[1024,400]{1,0:T(8,128)} %get-tuple-element.444, s32[]{:T(128)S(6)} %select_n.125), kind=kOutput, calls=%fused_computation.77.clone.1 | convolution fusion | flops 2458111488 | bytes 5146628 | tf_op jit(solution)/shard_map/while/body/eval_jaxpr/dot_general | solution.py:43
  138.3 4.9 %fusion.46 = f32[1000,400]{1,0:T(8,128)} fusion(f32[512,1000]{0,1:T(8,128)S(1)} %get-tuple-element.407, f32[512]{0:T(512)S(1)} %get-tuple-element.408, f32[512]{0:T(512)S(1)} %get-tuple-element.409, f32[1024,400]{1,0:T(8,128)S(1)} %copy-done.5, s32[]{:T(128)S(6)} %select_n.125), kind=kOutput, calls=%fused_computation.14.clone.1 | convolution fusion | flops 2458624000 | bytes 4700676 | tf_op jit(solution)/shard_map/while/body/eval_jaxpr/dot_general | solution.py:53
  143.2 10.1 %scatter_fusion = f32[1024,400]{1,0:T(8,128)} fusion(f32[1024,400]{1,0:T(8,128)} %get-tuple-element.429, s32[1000]{0:T(1024)S(1)} %bitcast.49, f32[1000,400]{1,0:T(8,128)} %fusion.46), kind=kCustom, calls=%fused_computation.6.clone.1 | custom fusion | flops 400000 | bytes 4804000 | tf_op jit(solution)/shard_map/while/body/eval_jaxpr/scatter-add | solution.py:109
  155.0 4.9 %gather_fusion = f32[1000,400]{1,0:T(8,128)} fusion(f32[1024,400]{1,0:T(8,128)S(1)} %get-tuple-element.447, s32[1024]{0:T(1024)S(1)} %pad_clamp_fusion.2), kind=kCustom, calls=%fused_computation.clone.1 | custom fusion | bytes 3204000 | tf_op jit(solution)/shard_map/while/body/eval_jaxpr/gather | solution.py:103
  159.9 5.4 %fusion.44 = (f32[512]{0:T(512)S(1)}, f32[512,1000]{0,1:T(8,128)S(1)}) fusion(f32[1000,400]{1,0:T(8,128)} %gather_fusion, f32[1024,400]{1,0:T(8,128)} %get-tuple-element.444, s32[]{:T(128)S(6)} %select_n.125), kind=kOutput, calls=%fused_computation.77.clone.1 | convolution fusion | flops 2458111488 | bytes 5146628 | tf_op jit(solution)/shard_map/while/body/eval_jaxpr/dot_general | solution.py:43
  172.4 4.9 %fusion.46 = f32[1000,400]{1,0:T(8,128)} fusion(f32[512,1000]{0,1:T(8,128)S(1)} %get-tuple-element.407, f32[512]{0:T(512)S(1)} %get-tuple-element.408, f32[512]{0:T(512)S(1)} %get-tuple-element.409, f32[1024,400]{1,0:T(8,128)S(1)} %copy-done.5, s32[]{:T(128)S(6)} %select_n.125), kind=kOutput, calls=%fused_computation.14.clone.1 | convolution fusion | flops 2458624000 | bytes 4700676 | tf_op jit(solution)/shard_map/while/body/eval_jaxpr/dot_general | solution.py:53
  177.2 10.1 %scatter_fusion = f32[1024,400]{1,0:T(8,128)} fusion(f32[1024,400]{1,0:T(8,128)} %get-tuple-element.429, s32[1000]{0:T(1024)S(1)} %bitcast.49, f32[1000,400]{1,0:T(8,128)} %fusion.46), kind=kCustom, calls=%fused_computation.6.clone.1 | custom fusion | flops 400000 | bytes 4804000 | tf_op jit(solution)/shard_map/while/body/eval_jaxpr/scatter-add | solution.py:109
  187.5 10.6 %scatter_custom_fusion.3 = f32[1024,400]{1,0:T(8,128)} fusion(f32[1024,400]{1,0:T(8,128)} %get-tuple-element.250, s32[1024]{0:T(1024)S(1)} %get-tuple-element.336, f32[1024]{0:T(1024)S(1)} %get-tuple-element.248, f32[1024,200]{1,0:T(8,128)} %copy-done.9, f32[1024,200]{1,0:T(8,128)S(1)} %get-tuple-element.330), kind=kCustom, calls=%fused_computation.43 | custom fusion | flops 1228800 | bytes 3739648 | tf_op jit(solution)/shard_map/scatter-add | solution.py:120
  200.9 4.3 all-to-all-start.3
  213.6 8.1 %scatter_custom_fusion.1 = f32[1024,400]{1,0:T(8,128)S(1)} fusion(s32[1024]{0:T(1024)S(1)} %get-tuple-element.339, f32[1024,200]{1,0:T(8,128)S(1)} %get-tuple-element.332, f32[]{:T(128)} %constant.108, f32[1024,200]{1,0:T(8,128)} %get-tuple-element.333, f32[]{:T(128)} %constant.97.clone.1), kind=kCustom, calls=%fused_computation.35 | custom fusion | flops 819200 | bytes 3506184 | tf_op jit(solution)/shard_map/scatter-add | solution.py:124
  223.5 21.0 %all-to-all-done.3 = f32[8,128,400]{1,2,0:T(8,128)} async-done(((f32[8,128,400]{1,2,0:T(8,128)}), f32[8,128,400]{1,2,0:T(8,128)}, u32[]{:S(2)}, u32[]{:S(2)}) %all-to-all-start.3) | async-done | bytes 1638432 | tf_op jit(solution)/shard_map/all_to_all | solution.py:145
  248.8 9.0 %scatter_custom_fusion.5 = f32[1345,400]{1,0:T(8,128)} fusion(s32[1024]{0:T(1024)S(1)} %get-tuple-element.334, f32[1024,200]{1,0:T(8,128)S(1)} %copy-done.13, f32[]{:T(128)} %constant.108, f32[1024,200]{1,0:T(8,128)S(1)} %copy-done.12, f32[]{:T(128)} %constant.97.clone.1), kind=kCustom, calls=%fused_computation.39 | custom fusion | flops 819200 | bytes 4249160 | tf_op jit(solution)/shard_map/scatter-add | solution.py:129
  260.3 155.8 %all-reduce.2.cloned.1.call-done = f32[1345,400]{1,0:T(8,128)} async-done(((f32[1345,400]{1,0:T(8,128)}), f32[1345,400]{1,0:T(8,128)}) %all-reduce.2.cloned.1.call-update) | async-done | bytes 2152016 | tf_op jit(solution)/shard_map/psum | solution.py:131
  427.1 6.8 %scatter_custom_fusion.2 = f32[512,400]{1,0:T(8,128)S(1)} fusion(s32[1024]{0:T(1024)S(1)} %bitcast.53, f32[1024,400]{1,0:T(8,128)S(1)} %bitcast.47, f32[]{:T(128)} %constant.97.clone.1), kind=kCustom, calls=%fused_computation.57 | custom fusion | flops 409600 | bytes 819204 | tf_op jit(solution)/shard_map/scatter-add | solution.py:142
  436.8 7.8 %scatter_fusion.1 = f32[512,400]{1,0:T(8,128)S(1)} fusion(f32[512,400]{1,0:T(8,128)S(1)} %scatter_custom_fusion.2, s32[1024]{0:T(1024)S(1)} %bitcast.50, f32[1024,400]{1,0:T(8,128)} %bitcast.43), kind=kCustom, calls=%fused_computation.10 | custom fusion | flops 409600 | bytes 4919296 | tf_op jit(solution)/shard_map/scatter-add | solution.py:149
  (115 shorter events, 83.0 us)
Async XLA Ops:
  8.6 12.5 %copy-start = (f32[512,400]{1,0:T(8,128)}, f32[512,400]{1,0:T(8,128)S(1)}, u32[]{:S(2)}) copy-start(f32[512,400]{1,0:T(8,128)S(1)} %copy.62) | copy-start | bytes 2457604
  14.6 6.5 %copy-start.16 = (s32[1,8,128]{2,1,0:T(8,128)S(1)}, s32[1,8,128]{2,1,0:T(8,128)}, u32[]{:S(2)}) copy-start(s32[1,8,128]{2,1,0:T(8,128)} %param.18) | copy-start | bytes 12292
  14.6 50.3 %all-to-all-start = ((f32[8,128,400]{1,2,0:T(8,128)}), f32[8,128,400]{1,2,0:T(8,128)}, u32[]{:S(2)}, u32[]{:S(2)}) async-start(f32[8,128,400]{1,2,0:T(8,128)} %copy.47), calls=%async_computation | async-start | bytes 3276800 | tf_op jit(solution)/shard_map/all_to_all | solution.py:82
  26.4 38.5 %collective-permute-start = (f32[8,128,400]{1,2,0:T(8,128)}, f32[8,128,400]{1,2,0:T(8,128)}, u32[]{:S(2)}, u32[]{:S(2)}) collective-permute-start(f32[8,128,400]{1,2,0:T(8,128)} %copy.51), channel_id=1, source_target_pairs={{0,24},{8,0},{16,8},{24,16},{1,25},{9,1},{17,9},{25,17},{2,26},{10... | collective-permute-start | bytes 4915208 | tf_op jit(solution)/shard_map/ppermute | solution.py:12
  64.9 44.0 %all-to-all-start.1 = ((f32[8,128,400]{1,2,0:T(8,128)}), f32[8,128,400]{1,2,0:T(8,128)}, u32[]{:S(2)}, u32[]{:S(2)}) async-start(f32[8,128,400]{1,2,0:T(8,128)} %collective-permute-done), calls=%async_computation.1 | async-start | bytes 3276800 | tf_op jit(solution)/shard_map/all_to_all | solution.py:87
  69.6 3.2 copy-start.18
  72.1 5.6 %copy-start.3 = (f32[1345,400]{1,0:T(8,128)}, f32[1345,400]{1,0:T(8,128)S(1)}, u32[]{:S(2)}) copy-start(f32[1345,400]{1,0:T(8,128)S(1)} %copy.49) | copy-start | bytes 6456004
  72.8 4.9 %copy-start.19 = (s32[1024]{0:T(1024)S(1)}, s32[1024]{0:T(1024)}, u32[]{:S(2)}) copy-start(s32[1024]{0:T(1024)} %param.19) | copy-start | bytes 12292
  72.8 4.9 %copy-start.20 = (s32[1024]{0:T(1024)S(1)}, s32[1024]{0:T(1024)}, u32[]{:S(2)}) copy-start(s32[1024]{0:T(1024)} %param.21) | copy-start | bytes 12292
  125.8 6.1 %copy-start.10 = (f32[1024,400]{0,1:T(8,128)S(1)}, f32[1024,400]{0,1:T(8,128)}, u32[]{:S(2)}) copy-start(f32[1024,400]{0,1:T(8,128)} %get-tuple-element.428) | copy-start | bytes 4915204 | tf_op jit(solution)/shard_map/while
  132.8 5.5 %copy-start.5 = (f32[1024,400]{1,0:T(8,128)S(1)}, f32[1024,400]{1,0:T(8,128)}, u32[]{:S(2)}) copy-start(f32[1024,400]{1,0:T(8,128)} %get-tuple-element.444) | copy-start | bytes 4915204 | tf_op jit(solution)/shard_map/while
  159.9 6.1 %copy-start.10 = (f32[1024,400]{0,1:T(8,128)S(1)}, f32[1024,400]{0,1:T(8,128)}, u32[]{:S(2)}) copy-start(f32[1024,400]{0,1:T(8,128)} %get-tuple-element.428) | copy-start | bytes 4915204 | tf_op jit(solution)/shard_map/while
  166.9 5.5 %copy-start.5 = (f32[1024,400]{1,0:T(8,128)S(1)}, f32[1024,400]{1,0:T(8,128)}, u32[]{:S(2)}) copy-start(f32[1024,400]{1,0:T(8,128)} %get-tuple-element.444) | copy-start | bytes 4915204 | tf_op jit(solution)/shard_map/while
  187.5 10.6 %copy-start.21 = (f32[1024]{0:T(1024)}, f32[1024]{0:T(1024)S(1)}, u32[]{:S(2)}) copy-start(f32[1024]{0:T(1024)S(1)} %get-tuple-element.300) | copy-start | bytes 12292
  200.9 43.5 %all-to-all-start.3 = ((f32[8,128,400]{1,2,0:T(8,128)}), f32[8,128,400]{1,2,0:T(8,128)}, u32[]{:S(2)}, u32[]{:S(2)}) async-start(f32[8,128,400]{1,2,0:T(8,128)} %copy.59), calls=%async_computation.3 | async-start | bytes 3276800 | tf_op jit(solution)/shard_map/all_to_all | solution.py:145
  223.5 25.3 %copy-start.12 = (f32[1024,200]{1,0:T(8,128)S(1)}, f32[1024,200]{1,0:T(8,128)}, u32[]{:S(2)}) copy-start(f32[1024,200]{1,0:T(8,128)} %get-tuple-element.326) | copy-start | bytes 2457604
  223.5 25.3 %copy-start.13 = (f32[1024,200]{1,0:T(8,128)S(1)}, f32[1024,200]{1,0:T(8,128)}, u32[]{:S(2)}) copy-start(f32[1024,200]{1,0:T(8,128)} %get-tuple-element.327) | copy-start | bytes 2457604
  244.4 180.8 %all-to-all-start.2 = ((f32[8,128,400]{1,2,0:T(8,128)}), f32[8,128,400]{1,2,0:T(8,128)}, u32[]{:S(2)}, u32[]{:S(2)}) async-start(f32[8,128,400]{1,2,0:T(8,128)} %copy.55), calls=%async_computation.2 | async-start | bytes 3276800 | tf_op jit(solution)/shard_map/all_to_all | solution.py:132
  248.7 167.4 %all-reduce.2.cloned.1.call-start = ((), (), s32[]{:S(2)}) async-start(), calls=%async_computation.4 | async-start | bytes 5537792 | tf_op jit(solution)/shard_map/psum | solution.py:131
  257.8 160.4 %copy-start.17 = (f32[1345]{0:T(1024)S(1)}, f32[1345]{0:T(1024)}, u32[]{:S(2)}) copy-start(f32[1345]{0:T(1024)} %param.16) | copy-start | bytes 16144
  257.8 160.4 %copy-start.4 = (f32[1345,400]{1,0:T(8,128)S(1)}, f32[1345,400]{1,0:T(8,128)}, u32[]{:S(2)}) copy-start(f32[1345,400]{1,0:T(8,128)} %copy-done.3) | copy-start | bytes 6456004
  257.8 176.1 %collective-permute-start.1 = (f32[8,128,400]{1,2,0:T(8,128)}, f32[8,128,400]{1,2,0:T(8,128)}, u32[]{:S(2)}, u32[]{:S(2)}) collective-permute-start(f32[8,128,400]{1,2,0:T(8,128)} %all-to-all-done.3), channel_id=1, source_target_pairs={{0,8},{8,16},{16,24},{24,0},{1,9},{9,17},{17,25},{25,1},{2,10},{10... | collective-permute-start | bytes 4915208 | tf_op jit(solution)/shard_map/ppermute | solution.py:12
  436.8 7.9 %copy-start.22 = (f32[512]{0:T(512)S(1)}, f32[512]{0:T(512)}, u32[]{:S(2)}) copy-start(f32[512]{0:T(512)} %param.14) | copy-start | bytes 6148
  436.8 7.9 %copy-start.1 = (f32[512,400]{1,0:T(8,128)S(1)}, f32[512,400]{1,0:T(8,128)}, u32[]{:S(2)}) copy-start(f32[512,400]{1,0:T(8,128)} %copy-done) | copy-start | bytes 2457604
  (10 other events, 20.3 us)
Sparse Core Ops, SparseCore 0:
  257.9 158.1 all-reduce.1
where the time goes:
time: 458 us; the launch traced here: 453 us
  waiting for transfers between devices  231 us (50%)
  other arithmetic  83.6 us (18%)
  local copies, waits for them, and re-layouts  68.6 us (15%)
  matrix products  29 us (6%)
  starting transfers between devices  24.7 us (5%)
  between operations  15.3 us (3%)
    psum x1, waiting for transfers between devices, on_device(): relation_total = lax.psum(relation_part, ('group', 'shard'))  156 us
    ppermute x2, waiting for transfers between devices, passed_along(): lax.ppermute(value, axis, [(i, (i + by) % count) for i in range(count)])  36.1 us
    all_to_all x1, waiting for transfers between devices, on_device(): lax.all_to_all(target_blocks_grad, 'shard', split_axis=0, concat_axis=0,...  21 us
    scatter-add x2, other arithmetic, span_turn(): target_grad = target_grad.at[slots].add(negative_grad)  20.2 us
    all_to_all x1, waiting for transfers between devices, on_device(): lax.all_to_all(shifted, 'shard', split_axis=0, concat_axis=0, tiled=True)  18.4 us
    dot_general x2, matrix products, span_terms(): neg_score = jnp.dot(queries, negatives.T, precision=lax.Precision.HIGHEST)  10.9 us
    scatter-add x1, other arithmetic, on_device(): target_grad = target_grad.at[edge_target].add(pos_grad[:, None] * queries)  10.6 us
    unnamed x42, local copies, waits for them, and re-layouts  10.4 us
  transfers between devices with their start and end apart: 7, of which 4 were waited for; matrix products, arithmetic and copies ran while one was open for 15% of the time, Pallas kernels for 0%

commit v1 on v0

--- a/solution.py
+++ b/solution.py
@@ -128,7 +128,7 @@
         .at[edge_relation]
         .add(conj_product(query_grad, head_rows))
     )
-    relation_total = lax.psum(relation_part, ("group", "shard"))
+    relation_total = jnp.sum(lax.all_gather(relation_part, ("group", "shard")), axis=0)
     returned_source = lax.all_to_all(
         source_grad.reshape(peer_count, block_size, feature_count),
         "shard",

time: 458 us -> 692 us (1.51)
  waiting for transfers between devices: 231 us -> 449 us
  other arithmetic: 83.6 us -> 100 us
    all_gather x0 -> x1, waiting for transfers between devices: none -> 249 us  [on_device(): lax.all_gather(relation_part, ('group', 'shard'))]
    psum x1 -> x0, waiting for transfers between devices: 156 us -> none  [on_device(): relation_total = lax.psum(relation_part, ('group', 'shard'))]
    all_to_all x1, waiting for transfers between devices: 0.01 us -> 77.7 us  [on_device(): lax.all_to_all(source_grad.reshape(peer_count, block_size, feature_count)...]
    all_to_all x1, waiting for transfers between devices: 21 us -> 68.1 us  [on_device(): lax.all_to_all(target_blocks_grad, 'shard', split_axis=0, concat_axis=0,...]
    reduce_sum x0 -> x1, other arithmetic: none -> 22.3 us  [on_device(): jnp.sum(lax.all_gather(relation_part, ('group', 'shard')), axis=0)]
  transfers between devices with their start and end apart: 7 -> 7, of which waited for: 4 -> 5; matrix products, arithmetic and copies ran while one was open for 15% -> 9% of each run, Pallas kernels for 0% -> 0%
where the time goes in v1:
time: 692 us; the launch traced here: 687 us
  waiting for transfers between devices  449 us (65%)
  other arithmetic  100 us (14%)
  local copies, waits for them, and re-layouts  68.6 us (10%)
  matrix products  29 us (4%)
  starting transfers between devices  23.7 us (3%)
  between operations  15.3 us (2%)
    all_gather x1, waiting for transfers between devices, on_device(): lax.all_gather(relation_part, ('group', 'shard'))  249 us
    all_to_all x1, waiting for transfers between devices, on_device(): lax.all_to_all(source_grad.reshape(peer_count, block_size, feature_count)...  77.7 us
    all_to_all x1, waiting for transfers between devices, on_device(): lax.all_to_all(target_blocks_grad, 'shard', split_axis=0, concat_axis=0,...  68.1 us
    ppermute x2, waiting for transfers between devices, passed_along(): lax.ppermute(value, axis, [(i, (i + by) % count) for i in range(count)])  36.1 us
    reduce_sum x1, other arithmetic, on_device(): jnp.sum(lax.all_gather(relation_part, ('group', 'shard')), axis=0)  22.3 us
    scatter-add x2, other arithmetic, span_turn(): target_grad = target_grad.at[slots].add(negative_grad)  20.3 us
    all_to_all x1, waiting for transfers between devices, on_device(): lax.all_to_all(shifted, 'shard', split_axis=0, concat_axis=0, tiled=True)  18.1 us
  transfers between devices with their start and end apart: 7, of which 5 were waited for; matrix products, arithmetic and copies ran while one was open for 9% of the time, Pallas kernels for 0%

profile of v1, /device:TPU:0, one launch (start us, length us, event | category | flops | bytes accessed | tf_op | source)
XLA Modules:
  0.0 686.9 jit_solution(15464881955999056468)
XLA Ops:
  14.6 6.5 all-to-all-start
  28.8 36.1 %collective-permute-done = f32[8,128,400]{1,2,0:T(8,128)} collective-permute-done((f32[8,128,400]{1,2,0:T(8,128)}, f32[8,128,400]{1,2,0:T(8,128)}, u32[]{:S(2)}, u32[]{:S(2)}) %collective-permute-start) | collective-permute-done | bytes 1638432 | tf_op jit(solution)/shard_map/ppermute | solution.py:12
  72.9 4.9 gather_fusion.3
  79.7 4.9 gather_fusion.2
  90.8 18.1 %all-to-all-done.1 = f32[8,128,400]{1,2,0:T(8,128)} async-done(((f32[8,128,400]{1,2,0:T(8,128)}), f32[8,128,400]{1,2,0:T(8,128)}, u32[]{:S(2)}, u32[]{:S(2)}) %all-to-all-start.1) | async-done | bytes 1638432 | tf_op jit(solution)/shard_map/all_to_all | solution.py:87
  110.8 4.9 gather_fusion.5
  118.8 68.8 %while.21 = (s32[]{:T(128)}, f32[1024]{0:T(1024)S(1)}, f32[1024]{0:T(1024)S(1)}, f32[1024,400]{0,1:T(8,128)}, f32[1024,400]{1,0:T(8,128)}, /*index=5*/f32[1024,4...) while((s32[]{:T(128)}, f32[1024]{0:T(1024)S(1)}, ...), condition=%wide.region_5.0_spmd, body=%wide.region_0.0_spmd.sunk | while | flops 7377200640 | bytes 52573032 | solution.py:118
  121.0 4.9 gather_fusion
  125.9 5.4 fusion.44
  138.4 4.9 fusion.46
  143.2 10.1 %scatter_fusion = f32[1024,400]{1,0:T(8,128)} fusion(f32[1024,400]{1,0:T(8,128)} %get-tuple-element.429, s32[1000]{0:T(1024)S(1)} %bitcast.51, f32[1000,400]{1,0:T(8,128)} %fusion.46), kind=kCustom, calls=%fused_computation.6.clone.1 | custom fusion | flops 400000 | bytes 4804000 | tf_op jit(solution)/shard_map/while/body/eval_jaxpr/scatter-add | solution.py:109
  155.1 4.9 gather_fusion
  160.0 5.4 fusion.44
  172.5 4.9 fusion.46
  177.3 10.1 %scatter_fusion = f32[1024,400]{1,0:T(8,128)} fusion(f32[1024,400]{1,0:T(8,128)} %get-tuple-element.429, s32[1000]{0:T(1024)S(1)} %bitcast.51, f32[1000,400]{1,0:T(8,128)} %fusion.46), kind=kCustom, calls=%fused_computation.6.clone.1 | custom fusion | flops 400000 | bytes 4804000 | tf_op jit(solution)/shard_map/while/body/eval_jaxpr/scatter-add | solution.py:109
  196.3 8.4 %scatter_custom_fusion.5 = f32[1345,400]{1,0:T(8,128)S(1)} fusion(s32[1024]{0:T(1024)S(1)} %get-tuple-element.334, f32[1024,200]{1,0:T(8,128)} %get-tuple-element.327, f32[]{:T(128)} %constant.108, f32[1024,200]{1,0:T(8,128)} %get-tuple-element.326, f32[]{:T(128)} %constant.97.clone.1), kind=kCustom, calls=%fused_computation.39 | custom fusion | flops 819200 | bytes 3790408 | tf_op jit(solution)/shard_map/scatter-add | solution.py:129
  208.5 8.7 %scatter_custom_fusion.3 = f32[1024,400]{1,0:T(8,128)S(1)} fusion(f32[1024,400]{1,0:T(8,128)S(1)} %copy-done, s32[1024]{0:T(1024)S(1)} %get-tuple-element.336, f32[1024]{0:T(1024)S(1)} %get-tuple-element.248, f32[1024,200]{1,0:T(8,128)} %copy-done.9, f32[1024,200]{1,0:T(8,128)} %copy-done.8), kind=kCustom, calls=%fused_computation.43 | custom fusion | flops 1228800 | bytes 3280896 | tf_op jit(solution)/shard_map/scatter-add | solution.py:120
  223.5 8.1 %scatter_custom_fusion.1 = f32[1024,400]{1,0:T(8,128)S(1)} fusion(s32[1024]{0:T(1024)S(1)} %get-tuple-element.339, f32[1024,200]{1,0:T(8,128)S(1)} %copy-done.13, f32[]{:T(128)} %constant.108, f32[1024,200]{1,0:T(8,128)} %get-tuple-element.333, f32[]{:T(128)} %constant.97.clone.1), kind=kCustom, calls=%fused_computation.35 | custom fusion | flops 819200 | bytes 3506184 | tf_op jit(solution)/shard_map/scatter-add | solution.py:124
  233.5 68.1 %all-to-all-done.3 = f32[8,128,400]{1,2,0:T(8,128)} async-done(((f32[8,128,400]{1,2,0:T(8,128)}), f32[8,128,400]{1,2,0:T(8,128)}, u32[]{:S(2)}, u32[]{:S(2)}) %all-to-all-start.3) | async-done | bytes 1638432 | tf_op jit(solution)/shard_map/all_to_all | solution.py:145
  306.9 77.7 %all-to-all-done.2 = f32[8,128,400]{1,2,0:T(8,128)S(1)} async-done(((f32[8,128,400]{1,2,0:T(8,128)}), f32[8,128,400]{1,2,0:T(8,128)S(1)}, u32[]{:S(2)}, u32[]{:S(2)}) %all-to-all-start.2) | async-done | bytes 1638432 | tf_op jit(solution)/shard_map/all_to_all | solution.py:132
  386.4 7.5 %scatter_custom_fusion.2 = f32[512,400]{1,0:T(8,128)S(1)} fusion(s32[1024]{0:T(1024)S(1)} %bitcast.55, f32[1024,400]{1,0:T(8,128)} %bitcast.49, f32[]{:T(128)} %constant.97.clone.1), kind=kCustom, calls=%fused_computation.57 | custom fusion | flops 409600 | bytes 819712 | tf_op jit(solution)/shard_map/scatter-add | solution.py:142
  395.8 7.8 %scatter_fusion.1 = f32[512,400]{1,0:T(8,128)S(1)} fusion(f32[512,400]{1,0:T(8,128)S(1)} %scatter_custom_fusion.2, s32[1024]{0:T(1024)S(1)} %bitcast.52, f32[1024,400]{1,0:T(8,128)} %bitcast.45), kind=kCustom, calls=%fused_computation.10 | custom fusion | flops 409600 | bytes 4919296 | tf_op jit(solution)/shard_map/scatter-add | solution.py:149
  405.1 249.1 %all-gather.4.cloned.1.call-done = f32[32,1345,400]{1,2,0:T(8,128)} async-done(((f32[1,1345,400]{1,2,0:T(8,128)}), f32[32,1345,400]{1,2,0:T(8,128)}) %all-gather.4.cloned.1.call-update) | async-done | bytes 68864016 | tf_op jit(solution)/shard_map/all_gather | solution.py:131
  654.3 22.3 %reduce_sum.60 = f32[1345,400]{0,1:T(8,128)S(1)} reduce(f32[32,1345,400]{1,2,0:T(8,128)} %all-gather.4.cloned.1.call-done, f32[]{:T(128)} %constant.97.clone.1), dimensions={0}, to_apply=%region_12.0 | reduce | flops 16678000 | bytes 71016000 | tf_op jit(solution)/shard_map/reduce_sum | solution.py:131
  (116 shorter events, 87.2 us)
Async XLA Ops:
  8.6 12.5 %copy-start.1 = (f32[512,400]{1,0:T(8,128)}, f32[512,400]{1,0:T(8,128)S(1)}, u32[]{:S(2)}) copy-start(f32[512,400]{1,0:T(8,128)S(1)} %copy.58) | copy-start | bytes 2457604
  14.6 6.5 copy-start.16
  14.6 50.3 %all-to-all-start = ((f32[8,128,400]{1,2,0:T(8,128)}), f32[8,128,400]{1,2,0:T(8,128)}, u32[]{:S(2)}, u32[]{:S(2)}) async-start(f32[8,128,400]{1,2,0:T(8,128)} %copy.43), calls=%async_computation | async-start | bytes 3276800 | tf_op jit(solution)/shard_map/all_to_all | solution.py:82
  26.4 38.5 %collective-permute-start = (f32[8,128,400]{1,2,0:T(8,128)}, f32[8,128,400]{1,2,0:T(8,128)}, u32[]{:S(2)}, u32[]{:S(2)}) collective-permute-start(f32[8,128,400]{1,2,0:T(8,128)} %copy.47), channel_id=1, source_target_pairs={{0,24},{8,0},{16,8},{24,16},{1,25},{9,1},{17,9},{25,17},{2,26},{10... | collective-permute-start | bytes 4915208 | tf_op jit(solution)/shard_map/ppermute | solution.py:12
  64.9 44.0 %all-to-all-start.1 = ((f32[8,128,400]{1,2,0:T(8,128)}), f32[8,128,400]{1,2,0:T(8,128)}, u32[]{:S(2)}, u32[]{:S(2)}) async-start(f32[8,128,400]{1,2,0:T(8,128)} %collective-permute-done), calls=%async_computation.1 | async-start | bytes 3276800 | tf_op jit(solution)/shard_map/all_to_all | solution.py:87
  69.6 584.6 %all-gather.4.cloned.1.call-start = ((), (), s32[]{:S(2)}) async-start(), calls=%async_computation.4 | async-start | bytes 74342400 | tf_op jit(solution)/shard_map/all_gather | solution.py:131
  69.7 3.2 copy-start.18
  72.9 4.9 copy-start.19
  72.9 4.9 copy-start.20
  115.7 3.1 copy-start.14
  125.9 6.1 copy-start.11
  132.9 5.5 copy-start.4
  160.0 6.1 copy-start.11
  167.0 5.5 copy-start.4
  187.6 5.0 copy-start.21
  187.6 3.0 copy-start.5
  190.6 2.9 copy-start.7
  218.9 4.7 copy-start.13
  218.9 82.6 %all-to-all-start.3 = ((f32[8,128,400]{1,2,0:T(8,128)}), f32[8,128,400]{1,2,0:T(8,128)}, u32[]{:S(2)}, u32[]{:S(2)}) async-start(f32[8,128,400]{1,2,0:T(8,128)} %copy.55), calls=%async_computation.3 | async-start | bytes 3276800 | tf_op jit(solution)/shard_map/all_to_all | solution.py:145
  233.4 73.4 %copy-start.15 = (s32[1,8,128]{2,1,0:T(8,128)S(1)}, s32[1,8,128]{2,1,0:T(8,128)}, u32[]{:S(2)}) copy-start(s32[1,8,128]{2,1,0:T(8,128)} %param.17) | copy-start | bytes 12292
  301.5 83.1 %all-to-all-start.2 = ((f32[8,128,400]{1,2,0:T(8,128)}), f32[8,128,400]{1,2,0:T(8,128)S(1)}, u32[]{:S(2)}, u32[]{:S(2)}) async-start(f32[8,128,400]{1,2,0:T(8,128)} %copy.51), calls=%async_computation.2 | async-start | bytes 3276800 | tf_op jit(solution)/shard_map/all_to_all | solution.py:132
  305.1 88.9 %collective-permute-start.1 = (f32[8,128,400]{1,2,0:T(8,128)}, f32[8,128,400]{1,2,0:T(8,128)S(1)}, u32[]{:S(2)}, u32[]{:S(2)}) collective-permute-start(f32[8,128,400]{1,2,0:T(8,128)} %all-to-all-done.3), channel_id=1, source_target_pairs={{0,8},{8,16},{16,24},{24,0},{1,9},{9,17},{17,25},{25,1},{2,10},{10... | collective-permute-start | bytes 4915208 | tf_op jit(solution)/shard_map/ppermute | solution.py:12
  395.8 7.9 %copy-start.22 = (f32[512]{0:T(512)S(1)}, f32[512]{0:T(512)}, u32[]{:S(2)}) copy-start(f32[512]{0:T(512)} %param.14) | copy-start | bytes 6148
  395.8 7.9 %copy-start.2 = (f32[512,400]{1,0:T(8,128)S(1)}, f32[512,400]{1,0:T(8,128)}, u32[]{:S(2)}) copy-start(f32[512,400]{1,0:T(8,128)} %copy-done.1) | copy-start | bytes 2457604
  (10 other events, 14.1 us)
Sparse Core Ops, SparseCore 0:
  207.0 447.1 all-gather.3
